TPU v7x, 256 devices: a whole 4x4x8 slice. The times are simulated.
256 devices in a mesh: dp: 16 (over x, y), expert: 16 (over z, core).
Axes of the slice: x: 4, y: 4, z: 8, core: 2. Of those that a mesh axis runs over, the one named last changes fastest.
Arguments:
- hidden_in: bfloat16 [256, 2, 2880], P(('expert', 'dp')), may hold values from -6 to 6
- queries: bfloat16 [256, 2, 4096], P(('expert', 'dp')), may hold values from -2 to 2
- new_keys: bfloat16 [256, 2, 512], P(('expert', 'dp')), may hold values from -2 to 2
- new_values: bfloat16 [256, 2, 512], P(('expert', 'dp')), may hold values from -6 to 6
- key_cache: bfloat16 [256, 512, 512], P(('expert', 'dp')), may hold values from -2 to 2
- value_cache: bfloat16 [256, 512, 512], P(('expert', 'dp')), may hold values from -6 to 6
- prompt_lengths: int32 [256], P(('expert', 'dp')), may hold values from 64 to 512, as said below
- out_weight: bfloat16 [4096, 2880], P('expert'), may hold values from -0.375 to 0.375
- norm_gain: float32 [2880], replicated, may hold values from 0.1 to 1.9
- expert_ids: int32 [256, 2, 4], P('expert'), may hold values from 0 to 31, all different within a row; in each aligned block of 32 rows (0 to 31, 32 to 63, ..., all dimensions but the last counted through in order) at most 12 rows name the same one
- top_logits: bfloat16 [256, 2, 4], P('expert'), may hold values from -4 to 4
- gate_weight: bfloat16 [32, 2880, 2880], P('expert', None, 'dp'), may hold values from -0.109375 to 0.109375
- up_weight: bfloat16 [32, 2880, 2880], P('expert', None, 'dp'), may hold values from -0.109375 to 0.109375
- down_weight: bfloat16 [32, 2880, 2880], P('expert', 'dp'), may hold values from -0.109375 to 0.109375
Outputs:
- layer_out: bfloat16 [256, 2, 2880], P(('expert', 'dp'))
Inputs may be any that keep to these rules, and one draw needn't show every extreme that they name: `prompt_lengths`: some row has exactly 512 live slots. `expert_ids`: A row names 4 different experts at each position. Over the 16 rows held by one index of the expert axis and both positions, no expert is named more than 12 times, and in some such group one expert is named exactly 12 times.
All inputs are finite; a program needn't handle non-finite values.
Results may differ from a plain program's by a relative error of at most 0.02.
Values may be sent and summed in bfloat16 or wider, within the bound.
No kernel may reach another device: no remote copies, remote signals or barrier semaphores. Data moves between devices by JAX's collectives and lax.ppermute only.
A program may use at most 128 MiB of HBM per device.

v0:
```python
import jax
import jax.numpy as jnp
from jax import lax
from jax.sharding import PartitionSpec as P

HQ = 64
KVH = 8
HD = 64


def attend_single(query_rows, fresh_keys, fresh_values, cache_keys, cache_values, length):
    step_count = query_rows.shape[0]
    cache_len = cache_keys.shape[0]
    keys_all = jnp.concatenate([cache_keys, fresh_keys], axis=0).reshape(
        cache_len + step_count, KVH, HD
    )
    values_all = jnp.concatenate([cache_values, fresh_values], axis=0).reshape(
        cache_len + step_count, KVH, HD
    )
    query_heads = query_rows.reshape(step_count, KVH, HQ // KVH, HD)
    scores = (
        jnp.einsum("sgqe,kge->sgqk", query_heads, keys_all, preferred_element_type=jnp.float32)
        * 0.125
    )
    position = jnp.arange(cache_len + step_count, dtype=jnp.int32)
    step_ids = jnp.arange(step_count, dtype=jnp.int32)
    visible = (position[None, :] < length) | (position[None, :] >= cache_len) & (
        position[None, :] - cache_len <= step_ids[:, None]
    )
    exp_scores = jnp.where(visible[:, None, None, :], jnp.exp(scores), jnp.zeros_like(scores))
    attn_probs = (exp_scores / jnp.sum(exp_scores, axis=-1, keepdims=True)).astype(jnp.bfloat16)
    attended = jnp.einsum(
        "sgqk,kge->sgqe", attn_probs, values_all, preferred_element_type=jnp.float32
    )
    return attended.astype(jnp.bfloat16).reshape(step_count, HQ * HD)


def rms_normed(residual, norm_gain):
    inverse_rms = lax.rsqrt(jnp.mean(residual * residual, axis=-1, keepdims=True) + 1e-05)
    return (residual * inverse_rms * norm_gain).astype(jnp.bfloat16)


def swiglu_act(gate_vals, up_vals):
    return (gate_vals * jax.nn.sigmoid(1.702 * gate_vals) * (up_vals + 1.0)).astype(jnp.bfloat16)


def expert_partials(slot_block, gate_weight, up_weight, down_weight):
    results = []
    for local_expert in range(slot_block.shape[1]):
        row_block = slot_block[:, local_expert].reshape(-1, slot_block.shape[3])
        gate_vals = jnp.dot(
            row_block, gate_weight[local_expert], preferred_element_type=jnp.float32
        )
        up_vals = jnp.dot(row_block, up_weight[local_expert], preferred_element_type=jnp.float32)
        activated = swiglu_act(gate_vals, up_vals)
        partial_out = jnp.dot(
            activated, down_weight[local_expert], preferred_element_type=jnp.float32
        )
        results.append(
            partial_out.reshape(slot_block.shape[0], slot_block.shape[2], slot_block.shape[3])
        )
    return jnp.stack(results, axis=1)


def routing_tables(chosen_ids, chosen_logits, experts_all, capacity):
    flat_ids = chosen_ids.reshape(-1, chosen_ids.shape[-1])
    exp_logits = jnp.exp(chosen_logits.reshape(flat_ids.shape).astype(jnp.float32))
    mix_weights = exp_logits / jnp.sum(exp_logits, axis=-1, keepdims=True)
    labels = jnp.arange(experts_all, dtype=jnp.int32)
    match_int = (flat_ids[:, :, None] == labels[None, None, :]).astype(jnp.int32)
    hits_int = jnp.sum(match_int, axis=1)
    slot_int = jnp.cumsum(hits_int, axis=0) - hits_int
    places = jnp.arange(capacity, dtype=jnp.int32)
    select = (
        hits_int.T[:, None, :] * (slot_int.T[:, None, :] == places[None, :, None]).astype(jnp.int32)
    ).astype(jnp.float32)
    token_slots = jnp.take_along_axis(slot_int, flat_ids, axis=1)
    source_rows = flat_ids * capacity + token_slots
    return (select, source_rows, mix_weights)


def gathered_combine(returned_flat, source_rows, mix_weights):
    picked = jnp.take(returned_flat, source_rows.reshape(-1), axis=0)
    picked = picked.reshape(source_rows.shape[0], source_rows.shape[1], returned_flat.shape[1])
    return jnp.sum(picked * mix_weights[:, :, None], axis=1)


def on_device(
    hidden_in,
    queries,
    new_keys,
    new_values,
    key_cache,
    value_cache,
    prompt_lengths,
    out_weight,
    norm_gain,
    expert_ids,
    top_logits,
    gate_weight,
    up_weight,
    down_weight,
):
    row_dev = hidden_in.shape[0]
    step_count = hidden_in.shape[1]
    model_width = hidden_in.shape[2]
    per_index = gate_weight.shape[0]
    expert_group = lax.axis_size("expert")
    experts_all = per_index * expert_group
    attended = jax.vmap(attend_single)(
        queries, new_keys, new_values, key_cache, value_cache, prompt_lengths
    )
    by_heads = lax.all_to_all(attended, "expert", split_axis=2, concat_axis=0, tiled=True)
    projected = lax.psum_scatter(
        jnp.einsum("rsf,fd->rsd", by_heads, out_weight, preferred_element_type=jnp.float32).astype(
            jnp.bfloat16
        ),
        "expert",
        scatter_dimension=0,
        tiled=True,
    ).astype(jnp.float32)
    residual = hidden_in.astype(jnp.float32) + projected
    normed = rms_normed(residual, norm_gain)
    capacity = row_dev * step_count
    start_row = lax.axis_index("dp") * row_dev
    mine_ids = lax.dynamic_slice_in_dim(expert_ids, start_row, row_dev, 0)
    mine_logits = lax.dynamic_slice_in_dim(top_logits, start_row, row_dev, 0)
    select, source_rows, mix_weights = routing_tables(mine_ids, mine_logits, experts_all, capacity)
    dispatch = jnp.einsum(
        "xct,td->xcd",
        select.astype(jnp.bfloat16),
        normed.reshape(-1, model_width),
        preferred_element_type=jnp.float32,
    )
    dispatch = dispatch.astype(jnp.bfloat16).reshape(expert_group, per_index, capacity, model_width)
    arrived = lax.all_to_all(dispatch, "expert", split_axis=0, concat_axis=0, tiled=True)
    partials = expert_partials(
        lax.all_gather(arrived, "dp", axis=0, tiled=True), gate_weight, up_weight, down_weight
    )
    summed = lax.psum_scatter(
        partials.astype(jnp.bfloat16), "dp", scatter_dimension=0, tiled=True
    ).astype(jnp.float32)
    returned = lax.all_to_all(
        summed.astype(jnp.bfloat16), "expert", split_axis=0, concat_axis=0, tiled=True
    ).astype(summed.dtype)
    moe_flat = gathered_combine(
        returned.reshape(experts_all * capacity, model_width), source_rows, mix_weights
    )
    moe_out = moe_flat.reshape(row_dev, step_count, model_width)
    return (residual + moe_out).astype(jnp.bfloat16)


def solution(mesh):
    placed = (
        P(("expert", "dp"), None, None),
        P(("expert", "dp"), None, None),
        P(("expert", "dp"), None, None),
        P(("expert", "dp"), None, None),
        P(("expert", "dp"), None, None),
        P(("expert", "dp"), None, None),
        P(("expert", "dp")),
        P("expert", None),
        P(),
        P("expert", None, None),
        P("expert", None, None),
        P("expert", None, "dp"),
        P("expert", None, "dp"),
        P("expert", "dp", None),
    )
    return jax.shard_map(
        on_device,
        mesh=mesh,
        in_specs=placed,
        out_specs=P(("expert", "dp"), None, None),
        check_vma=False,
    )
```

profile of v0, /device:TPU:1, one launch (start us, length us, event | category | flops | bytes accessed | tf_op | source)
XLA Modules:
  0.0 473.7 jit_solution(13765269799745457546)
XLA Ops:
  10.8 3.8 copy.84
  15.1 23.5 %reduce.9 = bf16[4096,2]{1,0:T(8,128)(2,1)S(1)} reduce(bf16[4096,1,2]{2,1,0:T(2,128)(2,1)} %bitcast.98, bf16[]{:T(256)} %broadcast.314), dimensions={1}, to_apply=%bitcast.89.reduce_sub_computation | reduce | bytes 32770
  38.6 2.2 reshape.367
  40.8 10.0 %all-to-all-start = ((bf16[16,2,256]{2,1,0:T(2,128)(2,1)}), bf16[16,2,256]{2,1,0:T(2,128)(2,1)S(1)}, u32[]{:S(2)}, u32[]{:S(2)}) async-start(bf16[16,2,256]{2,1,0:T(2,128)(2,1)} %reshape.367), calls=%async_computation | async-start | bytes 32768 | tf_op jit(solution)/shard_map/all_to_all | solution.py:113
  51.2 6.9 %all-to-all-done = bf16[16,2,256]{2,1,0:T(2,128)(2,1)S(1)} async-done(((bf16[16,2,256]{2,1,0:T(2,128)(2,1)}), bf16[16,2,256]{2,1,0:T(2,128)(2,1)S(1)}, u32[]{:S(2)}, u32[]{:S(2)}) %all-to-all-start) | async-done | bytes 16416 | tf_op jit(solution)/shard_map/all_to_all | solution.py:113
  58.1 4.3 reshape.368
  62.4 4.6 copy.85
  69.1 99.8 %all-reduce.5.cloned.1.call-done = bf16[16,2,2880]{2,1,0:T(2,128)(2,1)} async-done(((bf16[16,2,2880]{2,1,0:T(2,128)(2,1)}), bf16[16,2,2880]{2,1,0:T(2,128)(2,1)}) %all-reduce.5.cloned.1.call-update) | async-done | bytes 184336
  172.3 20.3 %all_to_all.28 = bf16[16,2,2,2880]{3,2,1,0:T(2,128)(2,1)} all-to-all(bf16[16,2,2,2880]{3,2,1,0:T(2,128)(2,1)S(1)} %bitcast.101), channel_id=1, replica_groups=mesh['dp'=16,'expert'=16] {'expert'}, dimensions={0} | all-to-all | bytes 737280 | tf_op jit(solution)/shard_map/all_to_all | solution.py:136
  192.9 7.0 %fusion.36 = (bf16[1,2880,180]{1,0,2:T(2,128)(2,1)}, bf16[1,2880,180]{1,0,2:T(2,128)(2,1)}) fusion(bf16[2,2880,180]{1,0,2:T(2,128)(2,1)} %param.25), kind=kLoop, calls=%fused_computation.84 | loop fusion | bytes 4147200 | tf_op jit(solution)/shard_map/slice | solution.py:52
  199.9 4.2 fusion.37
  204.1 4.2 fusion.38
  208.3 46.0 %all-gather.2.cloned.1.call-done = bf16[256,2,2,2880]{3,2,1,0:T(2,128)(2,1)} async-done(((bf16[16,2,2,2880]{3,2,1,0:T(2,128)(2,1)}), bf16[256,2,2,2880]{3,2,1,0:T(2,128)(2,1)}) %all-gather.2.cloned.1.call-update) | async-done | bytes 5898256 | tf_op jit(solution)/shard_map/all_gather | solution.py:138
  254.4 8.2 %fusion.35 = (bf16[256,1,2,2880]{3,2,1,0:T(2,128)(2,1)}, bf16[256,1,2,2880]{3,2,1,0:T(2,128)(2,1)}) fusion(bf16[256,2,2,2880]{3,2,1,0:T(2,128)(2,1)} %all-gather.2.cloned.1.call-done), kind=kLoop, calls=%fused_computation.83 | loop fusion | bytes 11796480 | tf_op jit(solution)/shard_map/slice | solution.py:50
  262.6 7.2 %reshape_squeeze.6 = bf16[512,2880]{1,0:T(8,128)(2,1)} reshape(bf16[256,1,2,2880]{3,2,1,0:T(2,128)(2,1)} %get-tuple-element.7) | data formatting | bytes 5898240 | tf_op jit(solution)/shard_map/reshape;squeeze | solution.py:50
  269.7 7.1 %reshape_squeeze.7 = bf16[512,2880]{1,0:T(8,128)(2,1)} reshape(bf16[256,1,2,2880]{3,2,1,0:T(2,128)(2,1)} %get-tuple-element.8) | data formatting | bytes 5898240 | tf_op jit(solution)/shard_map/reshape;squeeze | solution.py:50
  276.9 3.8 fusion.12
  282.4 3.8 fusion.11
  287.9 2.8 fusion
  291.8 3.0 pad_maximum_fusion
  294.8 15.6 %copy.98 = bf16[256,2,2,2880]{3,2,1,0:T(2,128)(2,1)} copy(bf16[256,2,2,2880]{0,3,2,1:T(8,128)(2,1)} %pad_maximum_fusion) | data formatting | bytes 11796480 | tf_op jit(solution)/shard_map/stack | solution.py:62
  313.4 127.0 %all-reduce.7.cloned.1.call-done = bf16[256,2,2,2880]{3,2,1,0:T(2,128)(2,1)} async-done(((bf16[256,2,2,2880]{3,2,1,0:T(2,128)(2,1)}), bf16[256,2,2,2880]{3,2,1,0:T(2,128)(2,1)}) %all-reduce.7.cloned.1.call-update) | async-done | bytes 5898256
  442.3 7.7 %all-to-all-start.2 = ((bf16[16,2,2,2880]{3,2,1,0:T(2,128)(2,1)}), bf16[16,2,2,2880]{3,2,1,0:T(2,128)(2,1)S(1)}, u32[]{:S(2)}, u32[]{:S(2)}) async-start(bf16[16,2,2,2880]{3,2,1,0:T(2,128)(2,1)} %constant_dynamic-slice_fusion), calls=%async_computation.2 | async-start | bytes 753664 | tf_op jit(solution)/shard_map/all_to_all | solution.py:143
  450.1 14.1 %all-to-all-done.2 = bf16[16,2,2,2880]{3,2,1,0:T(2,128)(2,1)S(1)} async-done(((bf16[16,2,2,2880]{3,2,1,0:T(2,128)(2,1)}), bf16[16,2,2,2880]{3,2,1,0:T(2,128)(2,1)S(1)}, u32[]{:S(2)}, u32[]{:S(2)}) %all-to-all-start.2) | async-done | bytes 368672 | tf_op jit(solution)/shard_map/all_to_all | solution.py:143
  (89 shorter events, 21.5 us)
Async XLA Ops:
  6.5 60.5 %copy-start = (bf16[256,2880]{0,1:T(8,128)(2,1)S(1)}, bf16[256,2880]{0,1:T(8,128)(2,1)}, u32[]{:S(2)}) copy-start(bf16[256,2880]{0,1:T(8,128)(2,1)} %param.21) | copy-start | bytes 4423684
  6.5 3.0 copy-start.9
  6.5 3.0 copy-start.13
  15.1 35.7 %copy-start.12 = (s32[16,2,4]{0,2,1:T(4,128)S(1)}, s32[16,2,4]{0,2,1:T(4,128)}, u32[]{:S(2)}) copy-start(s32[16,2,4]{0,2,1:T(4,128)} %param.23) | copy-start | bytes 1540
  40.8 17.3 %all-to-all-start = ((bf16[16,2,256]{2,1,0:T(2,128)(2,1)}), bf16[16,2,256]{2,1,0:T(2,128)(2,1)S(1)}, u32[]{:S(2)}, u32[]{:S(2)}) async-start(bf16[16,2,256]{2,1,0:T(2,128)(2,1)} %reshape.367), calls=%async_computation | async-start | bytes 32768 | tf_op jit(solution)/shard_map/all_to_all | solution.py:113
  50.8 118.2 %all-reduce.5.cloned.1.call-start = ((), (), s32[]{:S(2)}) async-start(), calls=%async_computation.4 | async-start | bytes 376832
  62.4 6.1 %copy-start.16 = (u32[256]{0:T(256)S(1)}, u32[256]{0:T(256)}, u32[]{:S(2)}) copy-start(u32[256]{0:T(256)} %constant.88) | copy-start | bytes 3076
  62.4 106.5 %copy-start.10 = (bf16[1,2,2880]{2,1,0:T(2,128)(2,1)S(1)}, bf16[1,2,2880]{2,1,0:T(2,128)(2,1)}, u32[]{:S(2)}) copy-start(bf16[1,2,2880]{2,1,0:T(2,128)(2,1)} %param.14) | copy-start | bytes 34564
  62.4 107.9 %copy-start.11 = (f32[2880]{0:T(1024)S(1)}, f32[2880]{0:T(1024)}, u32[]{:S(2)}) copy-start(f32[2880]{0:T(1024)} %param.22) | copy-start | bytes 34564
  68.4 185.9 %all-gather.2.cloned.1.call-start = ((), (), s32[]{:S(2)}) async-start(), calls=%async_computation.3 | async-start | bytes 6406144 | tf_op jit(solution)/shard_map/all_gather | solution.py:138
  192.6 247.7 %all-reduce.7.cloned.1.call-start = ((), (), s32[]{:S(2)}) async-start(), calls=%async_computation.5 | async-start | bytes 12058624
  192.9 7.0 %copy-start.2 = (bf16[2,2880,180]{1,0,2:T(2,128)(2,1)S(1)}, bf16[2,2880,180]{1,0,2:T(2,128)(2,1)}, u32[]{:S(2)}) copy-start(bf16[2,2880,180]{1,0,2:T(2,128)(2,1)} %param.26) | copy-start | bytes 6220804
  199.9 4.2 copy-start.3
  276.9 3.8 copy-start.6
  276.9 4.0 copy-start.8
  282.4 3.9 copy-start.5
  282.4 4.0 copy-start.7
  287.9 2.8 copy-start.4
  310.4 0.7 copy-start.15
  310.4 2.8 copy-start.14
  311.8 155.4 %copy-start.1 = (bf16[256,2880]{0,1:T(8,128)(2,1)S(1)}, bf16[256,2880]{0,1:T(8,128)(2,1)}, u32[]{:S(2)}) copy-start(bf16[256,2880]{0,1:T(8,128)(2,1)} %param.21) | copy-start | bytes 4423684
  442.3 21.9 %all-to-all-start.2 = ((bf16[16,2,2,2880]{3,2,1,0:T(2,128)(2,1)}), bf16[16,2,2,2880]{3,2,1,0:T(2,128)(2,1)S(1)}, u32[]{:S(2)}, u32[]{:S(2)}) async-start(bf16[16,2,2,2880]{3,2,1,0:T(2,128)(2,1)} %constant_dynamic-slice_fusion), calls=%async_computation.2 | async-start | bytes 753664 | tf_op jit(solution)/shard_map/all_to_all | solution.py:143
Sparse Core Ops, SparseCore 0:
  68.6 100.3 all-reduce.4
  192.8 61.5 all-gather.1
  310.6 129.7 all-reduce.6
where the time goes:
time: 475 us; the launch traced here: 474 us
  waiting for transfers between devices  294 us (62%)
  local copies, waits for them, and re-layouts  78.4 us (17%)
  other arithmetic  31.5 us (7%)
  blocking collectives  20.3 us (4%)
  starting transfers between devices  18 us (4%)
  matrix products  16.7 us (4%)
  between operations  14.9 us (3%)
    unnamed x5, waiting for transfers between devices  227 us
    all_gather x1, waiting for transfers between devices, on_device(): lax.all_gather(arrived, 'dp', axis=0, tiled=True)  46 us
    unnamed x1, other arithmetic  23.5 us
    all_to_all x1, blocking collectives, on_device(): lax.all_to_all(dispatch, 'expert', split_axis=0, concat_axis=0, tiled=True)  20.3 us
    another operation x1, local copies, waits for them, and re-layouts, expert_partials(): return jnp.stack(results, axis=1)  15.6 us
    another operation x2, local copies, waits for them, and re-layouts, expert_partials(): row_block = slot_block[:, local_expert].reshape(-1, slot_block.shape[3])  14.3 us
    all_to_all x1, waiting for transfers between devices, on_device(): lax.all_to_all(summed.astype(jnp.bfloat16), 'expert', split_axis=0, conca...  14.1 us
    unnamed x40, local copies, waits for them, and re-layouts  11.2 us
  transfers between devices with their start and end apart: 5, of which 5 were waited for; matrix products, arithmetic and copies ran while one was open for 4% of the time, Pallas kernels for 0%

commit v1 on v0

--- a/solution.py
+++ b/solution.py
@@ -110,7 +110,10 @@
     attended = jax.vmap(attend_single)(
         queries, new_keys, new_values, key_cache, value_cache, prompt_lengths
     )
-    by_heads = lax.all_to_all(attended, "expert", split_axis=2, concat_axis=0, tiled=True)
+    size = lax.axis_size("expert")
+    blocks = jnp.stack(jnp.split(attended, size, axis=2), axis=0)
+    blocks = lax.all_to_all(blocks, "expert", split_axis=0, concat_axis=0)
+    by_heads = jnp.concatenate(blocks, axis=0)
     projected = lax.psum_scatter(
         jnp.einsum("rsf,fd->rsd", by_heads, out_weight, preferred_element_type=jnp.float32).astype(
             jnp.bfloat16

time: 475 us -> 445 us (0.937)
  other arithmetic: 31.5 us -> 8.18 us
  local copies, waits for them, and re-layouts: 78.4 us -> 72.1 us
    unnamed x1 -> x0, other arithmetic: 23.5 us -> none
    unnamed x40 -> x52, local copies, waits for them, and re-layouts: 11.2 us -> 12.7 us
where the time goes in v1:
time: 445 us; the launch traced here: 444 us
  waiting for transfers between devices  294 us (66%)
  local copies, waits for them, and re-layouts  72.1 us (16%)
  blocking collectives  20.3 us (5%)
  starting transfers between devices  18 us (4%)
  matrix products  16.7 us (4%)
  between operations  14.9 us (3%)
  other arithmetic  8.18 us (2%)
    unnamed x5, waiting for transfers between devices  227 us
    all_gather x1, waiting for transfers between devices, on_device(): lax.all_gather(arrived, 'dp', axis=0, tiled=True)  45.9 us
    all_to_all x1, blocking collectives, on_device(): lax.all_to_all(dispatch, 'expert', split_axis=0, concat_axis=0, tiled=True)  20.3 us
    another operation x1, local copies, waits for them, and re-layouts, expert_partials(): return jnp.stack(results, axis=1)  15.6 us
    another operation x2, local copies, waits for them, and re-layouts, expert_partials(): row_block = slot_block[:, local_expert].reshape(-1, slot_block.shape[3])  14.3 us
    all_to_all x1, waiting for transfers between devices, on_device(): lax.all_to_all(summed.astype(jnp.bfloat16), 'expert', split_axis=0, conca...  14.1 us
    unnamed x52, local copies, waits for them, and re-layouts  12.7 us
    all_to_all x1, starting transfers between devices, on_device(): blocks = lax.all_to_all(blocks, 'expert', split_axis=0, concat_axis=0)  9.98 us
  transfers between devices with their start and end apart: 5, of which 5 were waited for; matrix products, arithmetic and copies ran while one was open for 4% of the time, Pallas kernels for 0%

profile of v1, /device:TPU:1, one launch (start us, length us, event | category | flops | bytes accessed | tf_op | source)
XLA Modules:
  0.0 443.9 jit_solution(9646688929630829948)
XLA Ops:
  19.9 10.0 %all-to-all-start = ((bf16[16,1,2,256]{3,2,1,0:T(2,128)(2,1)}), bf16[16,1,2,256]{3,2,1,0:T(2,128)(2,1)S(1)}, u32[]{:S(2)}, u32[]{:S(2)}) async-start(bf16[16,1,2,256]{3,2,1,0:T(2,128)(2,1)} %constant_dynamic-update-slice_fusion), calls=%async_computation | async-start | bytes 32768 | tf_op jit(solution)/shard_map/all_to_all | solution.py:115
  30.3 6.9 %all-to-all-done = bf16[16,1,2,256]{3,2,1,0:T(2,128)(2,1)S(1)} async-done(((bf16[16,1,2,256]{3,2,1,0:T(2,128)(2,1)}), bf16[16,1,2,256]{3,2,1,0:T(2,128)(2,1)S(1)}, u32[]{:S(2)}, u32[]{:S(2)}) %all-to-all-start) | async-done | bytes 16416 | tf_op jit(solution)/shard_map/all_to_all | solution.py:115
  39.3 99.6 %all-reduce.5.cloned.1.call-done = bf16[16,2,2880]{2,1,0:T(2,128)(2,1)} async-done(((bf16[16,2,2880]{2,1,0:T(2,128)(2,1)}), bf16[16,2,2880]{2,1,0:T(2,128)(2,1)}) %all-reduce.5.cloned.1.call-update) | async-done | bytes 184336
  139.0 1.5 multiply_reduce_fusion.1
  140.4 1.7 convolution_convert_fusion.2
  142.4 20.3 %all_to_all.15 = bf16[16,2,2,2880]{3,2,1,0:T(2,128)(2,1)} all-to-all(bf16[16,2,2,2880]{3,2,1,0:T(2,128)(2,1)S(1)} %bitcast.153), channel_id=1, replica_groups=mesh['dp'=16,'expert'=16] {'expert'}, dimensions={0} | all-to-all | bytes 737280 | tf_op jit(solution)/shard_map/all_to_all | solution.py:139
  163.0 7.1 %fusion.37 = (bf16[1,2880,180]{1,0,2:T(2,128)(2,1)}, bf16[1,2880,180]{1,0,2:T(2,128)(2,1)}) fusion(bf16[2,2880,180]{1,0,2:T(2,128)(2,1)} %param.25), kind=kLoop, calls=%fused_computation.116 | loop fusion | bytes 4147200 | tf_op jit(solution)/shard_map/slice | solution.py:52
  170.1 4.2 fusion.38
  174.3 4.2 fusion.39
  178.5 45.9 %all-gather.2.cloned.1.call-done = bf16[256,2,2,2880]{3,2,1,0:T(2,128)(2,1)} async-done(((bf16[16,2,2,2880]{3,2,1,0:T(2,128)(2,1)}), bf16[256,2,2,2880]{3,2,1,0:T(2,128)(2,1)}) %all-gather.2.cloned.1.call-update) | async-done | bytes 5898256 | tf_op jit(solution)/shard_map/all_gather | solution.py:141
  224.5 8.2 %fusion.36 = (bf16[256,1,2,2880]{3,2,1,0:T(2,128)(2,1)}, bf16[256,1,2,2880]{3,2,1,0:T(2,128)(2,1)}) fusion(bf16[256,2,2,2880]{3,2,1,0:T(2,128)(2,1)} %all-gather.2.cloned.1.call-done), kind=kLoop, calls=%fused_computation.115 | loop fusion | bytes 11796480 | tf_op jit(solution)/shard_map/slice | solution.py:50
  232.7 7.1 %reshape_squeeze.6 = bf16[512,2880]{1,0:T(8,128)(2,1)} reshape(bf16[256,1,2,2880]{3,2,1,0:T(2,128)(2,1)} %get-tuple-element.7) | data formatting | bytes 5898240 | tf_op jit(solution)/shard_map/reshape;squeeze | solution.py:50
  239.8 7.2 %reshape_squeeze.7 = bf16[512,2880]{1,0:T(8,128)(2,1)} reshape(bf16[256,1,2,2880]{3,2,1,0:T(2,128)(2,1)} %get-tuple-element.8) | data formatting | bytes 5898240 | tf_op jit(solution)/shard_map/reshape;squeeze | solution.py:50
  247.0 3.8 fusion.12
  251.0 1.2 fusion.7
  252.5 3.8 fusion.11
  258.1 2.8 fusion
  261.9 3.0 pad_maximum_fusion
  265.0 15.6 %copy.145 = bf16[256,2,2,2880]{3,2,1,0:T(2,128)(2,1)} copy(bf16[256,2,2,2880]{0,3,2,1:T(8,128)(2,1)} %pad_maximum_fusion) | data formatting | bytes 11796480 | tf_op jit(solution)/shard_map/stack | solution.py:62
  283.5 127.0 %all-reduce.7.cloned.1.call-done = bf16[256,2,2,2880]{3,2,1,0:T(2,128)(2,1)} async-done(((bf16[256,2,2,2880]{3,2,1,0:T(2,128)(2,1)}), bf16[256,2,2,2880]{3,2,1,0:T(2,128)(2,1)}) %all-reduce.7.cloned.1.call-update) | async-done | bytes 5898256
  410.5 2.0 constant_dynamic-slice_fusion
  412.5 7.7 %all-to-all-start.2 = ((bf16[16,2,2,2880]{3,2,1,0:T(2,128)(2,1)}), bf16[16,2,2,2880]{3,2,1,0:T(2,128)(2,1)S(1)}, u32[]{:S(2)}, u32[]{:S(2)}) async-start(bf16[16,2,2,2880]{3,2,1,0:T(2,128)(2,1)} %constant_dynamic-slice_fusion), calls=%async_computation.2 | async-start | bytes 753664 | tf_op jit(solution)/shard_map/all_to_all | solution.py:146
  420.3 14.1 %all-to-all-done.2 = bf16[16,2,2,2880]{3,2,1,0:T(2,128)(2,1)S(1)} async-done(((bf16[16,2,2,2880]{3,2,1,0:T(2,128)(2,1)}), bf16[16,2,2,2880]{3,2,1,0:T(2,128)(2,1)S(1)}, u32[]{:S(2)}, u32[]{:S(2)}) %all-to-all-start.2) | async-done | bytes 368672 | tf_op jit(solution)/shard_map/all_to_all | solution.py:146
  435.5 1.9 fusion.17
  (99 shorter events, 22.0 us)
Async XLA Ops:
  6.5 30.7 %copy-start = (bf16[256,2880]{0,1:T(8,128)(2,1)S(1)}, bf16[256,2880]{0,1:T(8,128)(2,1)}, u32[]{:S(2)}) copy-start(bf16[256,2880]{0,1:T(8,128)(2,1)} %param.21) | copy-start | bytes 4423684
  6.5 3.0 copy-start.9
  6.5 3.0 copy-start.13
  9.6 20.3 %copy-start.12 = (s32[16,2,4]{0,2,1:T(4,128)S(1)}, s32[16,2,4]{0,2,1:T(4,128)}, u32[]{:S(2)}) copy-start(s32[16,2,4]{0,2,1:T(4,128)} %param.23) | copy-start | bytes 1540
  10.3 28.5 %copy-start.16 = (u32[256]{0:T(256)S(1)}, u32[256]{0:T(256)}, u32[]{:S(2)}) copy-start(u32[256]{0:T(256)} %constant.88) | copy-start | bytes 3076
  10.3 128.7 %copy-start.10 = (bf16[1,2,2880]{2,1,0:T(2,128)(2,1)S(1)}, bf16[1,2,2880]{2,1,0:T(2,128)(2,1)}, u32[]{:S(2)}) copy-start(bf16[1,2,2880]{2,1,0:T(2,128)(2,1)} %param.14) | copy-start | bytes 34564
  10.3 130.2 %copy-start.11 = (f32[2880]{0:T(1024)S(1)}, f32[2880]{0:T(1024)}, u32[]{:S(2)}) copy-start(f32[2880]{0:T(1024)} %param.22) | copy-start | bytes 34564
  19.9 17.3 %all-to-all-start = ((bf16[16,1,2,256]{3,2,1,0:T(2,128)(2,1)}), bf16[16,1,2,256]{3,2,1,0:T(2,128)(2,1)S(1)}, u32[]{:S(2)}, u32[]{:S(2)}) async-start(bf16[16,1,2,256]{3,2,1,0:T(2,128)(2,1)} %constant_dynamic-update-slice_fusion), calls=%async_computation | async-start | bytes 32768 | tf_op jit(solution)/shard_map/all_to_all | solution.py:115
  29.9 109.0 %all-reduce.5.cloned.1.call-start = ((), (), s32[]{:S(2)}) async-start(), calls=%async_computation.4 | async-start | bytes 376832
  38.7 185.8 %all-gather.2.cloned.1.call-start = ((), (), s32[]{:S(2)}) async-start(), calls=%async_computation.3 | async-start | bytes 6406144 | tf_op jit(solution)/shard_map/all_gather | solution.py:141
  162.8 247.8 %all-reduce.7.cloned.1.call-start = ((), (), s32[]{:S(2)}) async-start(), calls=%async_computation.5 | async-start | bytes 12058624
  163.0 7.1 %copy-start.2 = (bf16[2,2880,180]{1,0,2:T(2,128)(2,1)S(1)}, bf16[2,2880,180]{1,0,2:T(2,128)(2,1)}, u32[]{:S(2)}) copy-start(bf16[2,2880,180]{1,0,2:T(2,128)(2,1)} %param.26) | copy-start | bytes 6220804
  170.1 4.2 copy-start.3
  247.0 3.8 copy-start.6
  247.0 4.0 copy-start.8
  252.5 3.9 copy-start.5
  252.5 4.0 copy-start.7
  258.1 2.8 copy-start.4
  280.6 0.7 copy-start.15
  280.6 2.8 copy-start.14
  281.9 155.5 %copy-start.1 = (bf16[256,2880]{0,1:T(8,128)(2,1)S(1)}, bf16[256,2880]{0,1:T(8,128)(2,1)}, u32[]{:S(2)}) copy-start(bf16[256,2880]{0,1:T(8,128)(2,1)} %param.21) | copy-start | bytes 4423684
  412.5 21.9 %all-to-all-start.2 = ((bf16[16,2,2,2880]{3,2,1,0:T(2,128)(2,1)}), bf16[16,2,2,2880]{3,2,1,0:T(2,128)(2,1)S(1)}, u32[]{:S(2)}, u32[]{:S(2)}) async-start(bf16[16,2,2,2880]{3,2,1,0:T(2,128)(2,1)} %constant_dynamic-slice_fusion), calls=%async_computation.2 | async-start | bytes 753664 | tf_op jit(solution)/shard_map/all_to_all | solution.py:146
Sparse Core Ops, SparseCore 0:
  38.8 100.1 all-reduce.4
  162.9 61.5 all-gather.1
  280.7 129.7 all-reduce.6
